TPU v7x, 256 devices: a whole 4x4x8 slice. The times are simulated.
256 devices in a mesh: row: 8 (over y, core), col: 32 (over x, z).
Axes of the slice: x: 4, y: 4, z: 8, core: 2. Of those that a mesh axis runs over, the one named last changes fastest.
Arguments:
- sources: float32 [65536, 256], P(('row', 'col')), may hold values from -6 to 6
- targets: float32 [65536, 256], P(('col', 'row')), may hold values from -6 to 6
- g_pot: float32 [65536], P(('col', 'row')), may hold values from -1 to 12
- log_a: float32 [65536], P(('row', 'col')), may hold values from -14 to -8
- log_b: float32 [65536], P(('col', 'row')), may hold values from -14 to -8
- src_block: int32 [16384], P(('row', 'col')), may hold values from 0 to 31, as said below
- tgt_block: int32 [16384], P(('row', 'col')), may hold values from 0 to 7, as said below
- pair_count: int32 [256], P(('row', 'col')), may hold values from 16 to 64, as said below
Outputs:
- f_new: float32 [65536], P(('row', 'col'))
- g_new: float32 [65536], P(('col', 'row'))
Inputs may be any that keep to these rules, and one draw needn't show every extreme that they name: `src_block`: within each row index, slot 0 of the 32 devices names together every source block of that row index once; slot k and slot k + 32 of a device name the same source block. `tgt_block`: within each col index, slot 0 of the 8 devices names together every target block of that col index once. `pair_count`: some device has all 64 slots live.
All inputs are finite; a program needn't handle non-finite values.
Results may differ from a plain program's by a relative error of at most 0.0003.
Values sent between devices are 32-bit elements; how exact they have to be, the bound alone decides.
A program may use at most 128 MiB of HBM per device.

v0:
```python
import functools
import math

import jax
import jax.numpy as jnp
from jax import lax
from jax.experimental import pallas as pl
from jax.experimental.pallas import tpu as pltpu
from jax.sharding import PartitionSpec as P

MESH = pl.DeviceIdType.MESH
BLK = 256
D = 256
ROWS = 264
NX, NY, NZ = 4, 4, 8
N_ROW, N_COL = 8, 32
ENTROPY = 0.05
LOG2E = 1.0 / math.log(2.0)
LN2 = math.log(2.0)
KAPPA = LOG2E / ENTROPY
LOWEST = -1.0e30
CHUNKS = ((0, 128), (128, 136))
VMEM_LIMIT = 60 * 1024 * 1024


def place():
    r, c = lax.axis_index("row"), lax.axis_index("col")
    return r // 2, lax.rem(r, 2), c // NZ, lax.rem(c, NZ)


def device(y, core, x, z):
    return {"row": y * 2 + core, "col": x * NZ + z}


def signal(sem, where):
    pl.semaphore_signal(sem, inc=1, device_id=where, device_id_type=MESH)


FIRST = ((1, 0), (3, 0), (0, 1), (0, 3))
SECOND = ((2, 0), (1, 1), (1, 3), (3, 1), (3, 3), (0, 2))
THIRD = ((2, 1), (2, 3), (1, 2), (3, 2))
FOURTH = ((2, 2),)


def sends_of(da, db):
    out = []
    if db == 0:
        if da == 0:
            out += [("A+", (1, 0)), ("A-", (3, 0))]
        if da == 1:
            out += [("A+", (2, 0))]
        out += [("B+", (da, 1)), ("B-", (da, 3))]
    elif db == 1 and da in (0, 1):
        out += [("B+", (da, 2))]
    elif db == 3 and da in (2, 3):
        out += [("B-", (da, 2))]
    return out


def gather_kernel(src_ref, tgt_ref, pot_ref, mass_ref, list_ref, x_out, y_out, lists_out,
                  load_sem, send_sem, recv_sem, mate_send, mate_recv, z_send, z_recv, l_send, l_recv):
    y, k, x, z = place()
    row = y * 2 + k

    def wrap4(v):
        return lax.rem(v + 8, 4)

    sigma = 1 - 2 * k

    def step_a(n):
        return wrap4(y + n * sigma * k), wrap4(x + n * sigma * (1 - k))

    def step_b(n):
        return wrap4(y + n * (1 - k)), wrap4(x + n * k)

    def dev_of(name):
        n = 1 if name[1] == "+" else -1
        ny, nx = step_a(n) if name[0] == "A" else step_b(n)
        return device(ny, k, nx, z)

    mate = device(y, 1 - k, x, z)
    z_long = device(y, k, x, lax.rem(z + sigma + NZ, NZ))
    z_short = device(y, k, x, lax.rem(z - sigma + NZ, NZ))

    def slot(da, db, core=None):
        if core is None:
            core = k
        oy = wrap4(y - db * (1 - core) + da * core)
        ox = wrap4(x - da * (1 - core) - db * core)
        return ox, oy * 2 + core

    loads = [
        pltpu.make_async_copy(tgt_ref, y_out.at[x, row, pl.ds(0, BLK)], load_sem.at[0]),
        pltpu.make_async_copy(pot_ref, y_out.at[x, row, pl.ds(BLK, 1)], load_sem.at[1]),
        pltpu.make_async_copy(src_ref, x_out.at[z, pl.ds(0, BLK)], load_sem.at[2]),
        pltpu.make_async_copy(mass_ref, x_out.at[z, pl.ds(BLK, 1)], load_sem.at[3]),
        pltpu.make_async_copy(list_ref, lists_out.at[x], load_sem.at[4]),
    ]
    for copy in loads:
        copy.start()
    barrier = pltpu.get_barrier_semaphore()
    peers = [device(y, k, wrap4(x + 1), z), device(y, k, wrap4(x + 3), z), device(y, k, wrap4(x + 2), z),
             device(wrap4(y + 1), k, x, z), device(wrap4(y + 3), k, x, z), mate, z_long, z_short]
    for peer in peers:
        signal(barrier, peer)
    pl.semaphore_wait(barrier, len(peers))
    for copy in loads:
        copy.wait()

    pending = []

    def at(pos):
        return pos[0] * 4 + pos[1]

    def part(ref, ch):
        return ref.at[pl.ds(*CHUNKS[ch])]

    def y_copy(pos, ch, where, target, n):
        ox, orow = slot(*pos)
        return pltpu.make_async_remote_copy(
            src_ref=part(y_out.at[ox, orow], ch), dst_ref=part(y_out.at[ox, orow], ch),
            send_sem=send_sem.at[at(pos), ch, n], recv_sem=recv_sem.at[at(target), ch],
            device_id=where, device_id_type=MESH)

    def mate_copy(pos, ch):
        ox, orow = slot(*pos)
        return pltpu.make_async_remote_copy(
            src_ref=part(y_out.at[ox, orow], ch), dst_ref=part(y_out.at[ox, orow], ch),
            send_sem=mate_send.at[at(pos), ch], recv_sem=mate_recv.at[at(pos), ch],
            device_id=mate, device_id_type=MESH)

    def send_y(pos, ch):
        for n, (name, target) in enumerate(sends_of(*pos)):
            copy = y_copy(pos, ch, dev_of(name), target, n)
            copy.start()
            pending.append(copy)
        copy = mate_copy(pos, ch)
        copy.start()
        pending.append(copy)

    def recv_y(pos, ch):
        ox, orow = slot(*pos)
        ref = part(y_out.at[ox, orow], ch)
        pltpu.make_async_remote_copy(src_ref=ref, dst_ref=ref, send_sem=send_sem.at[0, 0, 0],
                                     recv_sem=recv_sem.at[at(pos), ch], device_id=mate,
                                     device_id_type=MESH).wait_recv()

    def recv_mate(pos, ch):
        ox, orow = slot(*pos, core=1 - k)
        ref = part(y_out.at[ox, orow], ch)
        pltpu.make_async_remote_copy(src_ref=ref, dst_ref=ref, send_sem=send_sem.at[0, 0, 0],
                                     recv_sem=mate_recv.at[at(pos), ch], device_id=mate,
                                     device_id_type=MESH).wait_recv()

    def z_slot(n):
        return lax.rem(z - n * sigma + NZ * 4, NZ)

    def send_z(n, ch, long):
        target = n + 1 if long else n - 1
        ref = part(x_out.at[z_slot(n)], ch)
        copy = pltpu.make_async_remote_copy(
            src_ref=ref, dst_ref=ref, send_sem=z_send.at[n + 4, ch, 0 if long else 1],
            recv_sem=z_recv.at[target + 4, ch],
            device_id=z_long if long else z_short, device_id_type=MESH)
        copy.start()
        pending.append(copy)

    def recv_z(n, ch):
        ref = part(x_out.at[z_slot(n)], ch)
        pltpu.make_async_remote_copy(src_ref=ref, dst_ref=ref, send_sem=send_sem.at[0, 0, 0],
                                     recv_sem=z_recv.at[n + 4, ch], device_id=mate,
                                     device_id_type=MESH).wait_recv()

    for n in (1, 2, 3):
        copy = pltpu.make_async_remote_copy(
            src_ref=lists_out.at[x], dst_ref=lists_out.at[x], send_sem=l_send.at[n - 1], recv_sem=l_recv.at[n - 1],
            device_id=device(y, k, wrap4(x + n), z), device_id_type=MESH)
        copy.start()
        pending.append(copy)
    for ch in (0, 1):
        send_y((0, 0), ch)
        send_z(0, ch, True)
        send_z(0, ch, False)
    levels = (FIRST, SECOND, THIRD, FOURTH)
    for level in range(4):
        for ch in (0, 1):
            for pos in levels[level]:
                recv_y(pos, ch)
                send_y(pos, ch)
            n = level + 1
            recv_z(n, ch)
            if n < 4:
                send_z(n, ch, True)
                recv_z(-n, ch)
                if n < 3:
                    send_z(-n, ch, False)
    for n in (1, 2, 3):
        ref = lists_out.at[wrap4(x - n)]
        pltpu.make_async_remote_copy(src_ref=ref, dst_ref=ref, send_sem=l_send.at[0], recv_sem=l_recv.at[n - 1],
                                     device_id=mate, device_id_type=MESH).wait_recv()
    for ch in (0, 1):
        for da in range(4):
            for db in range(4):
                recv_mate((da, db), ch)
    for copy in pending:
        copy.wait_send()


def split3(v):
    hi = v.astype(jnp.bfloat16)
    lo = (v - hi.astype(jnp.float32)).astype(jnp.bfloat16)
    return hi, lo


def prep_kernel_body(x_raw, y_raw, x3, y3, bias):
    def one_x(i, carry):
        hi, lo = split3(x_raw[i, pl.ds(0, BLK), :])
        x3[i, :, pl.ds(0, D)] = hi
        x3[i, :, pl.ds(D, D)] = lo
        x3[i, :, pl.ds(2 * D, D)] = hi
        return carry

    lax.fori_loop(0, NZ, one_x, 0)

    def one_y(i, carry):
        block = y_raw[i, pl.ds(0, BLK), :].T
        pot = y_raw[i, pl.ds(BLK, 1), :]
        square = jnp.sum(block * block, axis=0, keepdims=True)
        row = KAPPA * (pot - square * (1.0 / D))
        bias[i] = jnp.broadcast_to(row, (8, BLK))
        hi, lo = split3(block * (2.0 * KAPPA / D))
        y3[i, pl.ds(0, D), :] = hi
        y3[i, pl.ds(D, D), :] = hi
        y3[i, pl.ds(2 * D, D), :] = lo
        return carry

    lax.fori_loop(0, NX * N_ROW, one_y, 0)


def pairs_of(lists, quarter, body):
    for other in range(NX):
        def one(i, carry, other=other):
            src = lists[other, 0, i]

            @pl.when(src // NZ == quarter)
            def _():
                body(lax.rem(src, NZ), other * N_ROW + lists[other, 0, 64 + i])
            return carry

        lax.fori_loop(0, lists[other, 1, 0], one, 0)


def first_kernel(lists, quarter, x_raw, y_raw, x3, y3, part_out, bias, top, total):
    prep_kernel_body(x_raw, y_raw, x3, y3, bias)
    top[...] = jnp.full(top.shape, LOWEST, jnp.float32)
    total[...] = jnp.zeros(total.shape, jnp.float32)

    def pair(b, t):
        g = jnp.dot(x3[b], y3[t], preferred_element_type=jnp.float32)
        row = bias[t]
        s1 = g[:, :128] + row[0:1, :128]
        s2 = g[:, 128:] + row[0:1, 128:]
        old = top[b]
        new = jnp.maximum(old, jnp.maximum(s1, s2))
        total[b] = total[b] * jnp.exp2(old - new) + jnp.exp2(s1 - new) + jnp.exp2(s2 - new)
        top[b] = new

    pairs_of(lists, quarter[0], pair)

    def close(b, carry):
        high = jnp.max(top[b], axis=1, keepdims=True)
        whole = jnp.sum(total[b] * jnp.exp2(top[b] - high), axis=1, keepdims=True)
        logs = jnp.where(whole > 0.0, high + jnp.log2(whole), LOWEST)
        part_out[b] = jnp.broadcast_to(logs, (BLK, 128)).T[0:8, :]
        return carry

    lax.fori_loop(0, NZ, close, 0)


def row_exchange_kernel(part_ref, x_raw, f_out, c_out, got, send_sem, recv_sem):
    y, k, x, z = place()
    barrier = pltpu.get_barrier_semaphore()
    for n in range(1, NZ):
        signal(barrier, device(y, k, x, lax.rem(z + n, NZ)))
    pl.semaphore_wait(barrier, NZ - 1)
    copies = []
    for n in range(1, NZ):
        copy = pltpu.make_async_remote_copy(
            src_ref=part_ref, dst_ref=got.at[n - 1], send_sem=send_sem.at[n - 1], recv_sem=recv_sem.at[n - 1],
            device_id=device(y, k, x, lax.rem(z + n, NZ)), device_id_type=MESH)
        copy.start()
        copies.append(copy)
    for copy in copies:
        copy.wait()
    own = part_ref[...]
    others = [got[n] for n in range(NZ - 1)]
    top = own
    for v in others:
        top = jnp.maximum(top, v)
    total = jnp.exp2(own - top)
    for v in others:
        total = total + jnp.exp2(v - top)
    logs = top + jnp.log2(total)
    c_out[...] = LOG2E * x_raw[:, pl.ds(BLK, 1), :] - logs
    square = x_raw[z, pl.ds(0, BLK), :].T
    square = jnp.sum(square * square, axis=0, keepdims=True)
    mass = x_raw[z, pl.ds(BLK, 1), :]
    c_here = c_out[z]
    f_out[...] = ENTROPY * mass - (ENTROPY * LN2) * (LOG2E * mass - c_here[0:1, :]) + square * (1.0 / D)


def second_kernel(lists, quarter, x3, y3, c_ref, part_out, cols, top, total):
    top[...] = jnp.full(top.shape, LOWEST, jnp.float32)
    total[...] = jnp.zeros(total.shape, jnp.float32)

    def widen(b, carry):
        cols[b] = jnp.broadcast_to(c_ref[b, pl.ds(0, 1), :], (128, BLK)).T
        return carry

    lax.fori_loop(0, NZ, widen, 0)

    def pair(b, t):
        g = jnp.dot(x3[b], y3[t], preferred_element_type=jnp.float32)
        col = cols[b]
        u = g + jnp.concatenate([col, col], axis=1)
        u = u.reshape(BLK // 8, 8, BLK)
        old = top[t]
        new = jnp.maximum(old, jnp.max(u, axis=0))
        total[t] = total[t] * jnp.exp2(old - new) + jnp.sum(jnp.exp2(u - new[None]), axis=0)
        top[t] = new

    pairs_of(lists, quarter[0], pair)

    def close(t, carry):
        high = jnp.max(top[t], axis=0, keepdims=True)
        whole = jnp.sum(total[t] * jnp.exp2(top[t] - high), axis=0, keepdims=True)
        part_out[t] = jnp.where(whole > 0.0, high + jnp.log2(whole), LOWEST)
        return carry

    lax.fori_loop(0, NX * N_ROW, close, 0)


def col_exchange_kernel(part_ref, tgt_ref, mass_ref, g_out, got, send_sem, recv_sem):
    y, k, x, z = place()
    me = x * N_ROW + y * 2 + k
    many = NX * N_ROW
    barrier = pltpu.get_barrier_semaphore()

    def peer(n):
        other = lax.rem(me + n, many)
        return other, {"row": lax.rem(other, N_ROW), "col": (other // N_ROW) * NZ + z}

    for n in range(1, many):
        signal(barrier, peer(n)[1])
    pl.semaphore_wait(barrier, many - 1)
    copies = []
    for n in range(1, many):
        other, where = peer(n)
        copy = pltpu.make_async_remote_copy(
            src_ref=part_ref.at[other], dst_ref=got.at[n], send_sem=send_sem.at[n], recv_sem=recv_sem.at[n],
            device_id=where, device_id_type=MESH)
        copy.start()
        copies.append(copy)
    block = tgt_ref[...].T
    square = jnp.sum(block * block, axis=0, keepdims=True)
    for copy in copies:
        copy.wait()
    got[0] = part_ref[me]
    every = got[...]
    top = jnp.max(every, axis=0)
    total = jnp.sum(jnp.exp2(every - top[None]), axis=0)
    logs = top + jnp.log2(total)
    g_out[...] = ENTROPY * mass_ref[...] - (ENTROPY * LN2) * logs + square * (1.0 / D)

def nt_dot(a, b):
    return lax.dot_general(a, b, (((1,), (1,)), ((), ())), preferred_element_type=jnp.float32)


def merged_kernel(src_list, tgt_list, count_ref, src_ref, tgt_ref, pot_ref, mass_ref, mass_b_ref,
                  f_out, g_out, bad_out,
                  y_raw, x_raw, y3, x3, bias, top, total, scores, col_top, col_sum, tabs, tab_s, mine, row_out, row_logs, row_got,
                  col_out, col_got,
                  load_sem, send_sem, recv_sem, mate_send, mate_recv, z_send, z_recv, l_send, l_recv,
                  row_send, row_recv, col_send, col_recv):
    y, k, x, z = place()
    row = y * 2 + k
    sigma = 1 - 2 * k

    def wrap4(v):
        return lax.rem(v + 8, 4)

    def step_a(n):
        return wrap4(y + n * sigma * k), wrap4(x + n * sigma * (1 - k))

    def step_b(n):
        return wrap4(y + n * (1 - k)), wrap4(x + n * k)

    def dev_of(name):
        n = 1 if name[1] == "+" else -1
        ny, nx = step_a(n) if name[0] == "A" else step_b(n)
        return device(ny, k, nx, z)

    mate = device(y, 1 - k, x, z)
    z_long = device(y, k, x, lax.rem(z + sigma + NZ, NZ))
    z_short = device(y, k, x, lax.rem(z - sigma + NZ, NZ))

    def slot(da, db, core):
        oy = wrap4(y - db * (1 - core) + da * core)
        ox = wrap4(x - da * (1 - core) - db * core)
        return ox, oy * 2 + core

    loads = [
        pltpu.make_async_copy(tgt_ref, y_raw.at[x, row, pl.ds(0, BLK)], load_sem.at[0]),
        pltpu.make_async_copy(pot_ref, y_raw.at[x, row, pl.ds(BLK, 1)], load_sem.at[1]),
        pltpu.make_async_copy(src_ref, x_raw.at[z, pl.ds(0, BLK)], load_sem.at[2]),
        pltpu.make_async_copy(mass_ref, x_raw.at[z, pl.ds(BLK, 1)], load_sem.at[3]),
    ]
    for copy in loads:
        copy.start()
    barrier = pltpu.get_barrier_semaphore()
    peers = [device(y, k, wrap4(x + 1), z), device(y, k, wrap4(x + 3), z), device(y, k, wrap4(x + 2), z),
             device(wrap4(y + 1), k, x, z), device(wrap4(y + 3), k, x, z), mate, z_long, z_short]
    for peer in peers:
        signal(barrier, peer)

    ids = lax.broadcasted_iota(jnp.int32, (N_COL, 128), 0)
    left = lax.broadcasted_iota(jnp.int32, (N_COL, 128), 1) < 64
    live = count_ref[0]

    def enter(i, carry):
        table, named = carry
        one = jnp.where(i < live, tgt_list[i] + 1, 0)
        two = jnp.where(i + 32 < live, tgt_list[i + 32] + 1, 0)
        here = ids == src_list[i]
        table = table + jnp.where(here, jnp.where(left, one, two), 0)
        named = named + jnp.where(here, jnp.where(i < live, 1, 0), 0)
        return table, named

    nothing = jnp.zeros((N_COL, 128), jnp.int32)
    table, named = lax.fori_loop(0, 32, enter, (nothing, nothing))
    mine[...] = jnp.minimum(table, N_ROW)
    bad = jnp.max(jnp.where(named > 1, 1.0, 0.0), axis=0, keepdims=True)
    top[...] = jnp.full(top.shape, LOWEST, jnp.float32)
    total[...] = jnp.zeros(total.shape, jnp.float32)

    pl.semaphore_wait(barrier, len(peers))
    for copy in loads:
        copy.wait()

    pending = []

    def at(pos):
        return pos[0] * 4 + pos[1]

    def part(ref, ch):
        return ref.at[pl.ds(*CHUNKS[ch])]

    def remote(src, dst, send, recv, where):
        return pltpu.make_async_remote_copy(src_ref=src, dst_ref=dst, send_sem=send, recv_sem=recv,
                                            device_id=where, device_id_type=MESH)

    def start(copy):
        copy.start()
        pending.append(copy)

    def arrived(ref, sem):
        remote(ref, ref, send_sem.at[0, 0, 0], sem, mate).wait_recv()

    def send_y(pos, ch):
        ref = part(y_raw.at[slot(*pos, k)], ch)
        for n, (name, target) in enumerate(sends_of(*pos)):
            start(remote(ref, ref, send_sem.at[at(pos), ch, n], recv_sem.at[at(target), ch], dev_of(name)))

    def send_mate(pos, ch):
        ref = part(y_raw.at[slot(*pos, k)], ch)
        start(remote(ref, ref, mate_send.at[at(pos), ch], mate_recv.at[at(pos), ch], mate))

    def recv_y(pos, ch):
        arrived(part(y_raw.at[slot(*pos, k)], ch), recv_sem.at[at(pos), ch])

    def z_slot(n):
        return lax.rem(z - n * sigma + NZ * 4, NZ)

    def send_z(n, ch, long):
        target = n + 1 if long else n - 1
        ref = part(x_raw.at[z_slot(n)], ch)
        start(remote(ref, ref, z_send.at[n + 4, ch, 0 if long else 1], z_recv.at[target + 4, ch],
                     z_long if long else z_short))

    def recv_z(n, ch):
        arrived(part(x_raw.at[z_slot(n)], ch), z_recv.at[n + 4, ch])

    def prep_x(zb):
        hi, lo = split3(x_raw[zb, pl.ds(0, BLK), :])
        x3[zb, :, pl.ds(0, D)] = hi
        x3[zb, :, pl.ds(D, D)] = lo
        x3[zb, :, pl.ds(2 * D, D)] = hi

    def prep_y(da, db, core):
        xq, t = slot(da, db, core)
        block = y_raw[xq, t, pl.ds(0, BLK), :]
        square = jnp.sum(block * block, axis=1, keepdims=True)
        square = jnp.broadcast_to(square, (BLK, 128)).T[0:8]
        bias[xq, t] = KAPPA * (y_raw[xq, t, pl.ds(BLK, 1), :] - square * (1.0 / D))
        hi, lo = split3(block * (2.0 * KAPPA / D))
        y3[xq, t, :, pl.ds(0, D)] = hi
        y3[xq, t, :, pl.ds(D, D)] = hi
        y3[xq, t, :, pl.ds(2 * D, D)] = lo

    def prep_mate(da, db):
        for ch in (0, 1):
            arrived(part(y_raw.at[slot(da, db, 1 - k)], ch), mate_recv.at[da * 4 + db, ch])
        prep_y(da, db, 1 - k)

    def prep_loop(many, pos):
        def one(i, carry):
            da, db = pos(i)
            prep_y(da, db, k)
            prep_mate(da, db)
            return carry

        lax.fori_loop(0, many, one, 0)

    def pair(xq, zb):
        parts = []
        for n in (0, 1):
            t = tab_s[xq, zb, 64 * n]
            alive = t > 0
            t = lax.max(t - 1, 0)
            g = nt_dot(x3[zb], y3[xq, t])
            scores[xq, n, zb] = g
            shift = jnp.where(alive, bias[xq, t], LOWEST)[0:1]
            parts += [g[:, :128] + shift[:, :128], g[:, 128:] + shift[:, 128:]]
        old = top[zb]
        new = jnp.maximum(old, jnp.maximum(jnp.maximum(parts[0], parts[1]), jnp.maximum(parts[2], parts[3])))
        e = [jnp.exp2(v - new) for v in parts]
        total[zb] = total[zb] * jnp.exp2(old - new) + ((e[0] + e[1]) + (e[2] + e[3]))
        top[zb] = new

    def pair_loop(many, which):
        def one(i, carry):
            pair(*which(i))
            return carry

        lax.fori_loop(0, many, one, 0)

    for ch in (0, 1):
        send_y((0, 0), ch)
        send_z(0, ch, True)
        send_z(0, ch, False)
        send_mate((0, 0), ch)
    keep = pltpu.make_async_copy(mine.at[pl.ds(x * NZ, NZ)], tabs.at[x], load_sem.at[0])
    keep.start()
    for n in (1, 2, 3):
        to = wrap4(x + n)
        start(remote(mine.at[pl.ds(to * NZ, NZ)], tabs.at[x], l_send.at[n - 1], l_recv.at[n - 1], device(y, k, to, z)))
    keep.wait()
    prep_x(z)
    prep_y(0, 0, k)

    levels = (FIRST, SECOND, THIRD, FOURTH)

    def events(level):
        n = level + 1
        for ch in (0, 1):
            for pos in levels[level]:
                recv_y(pos, ch)
                send_y(pos, ch)
                send_mate(pos, ch)
            recv_z(n, ch)
            if n < 4:
                send_z(n, ch, True)
                recv_z(-n, ch)
                if n < 3:
                    send_z(-n, ch, False)

    def prep_xs(n):
        def one(i, carry):
            prep_x(z_slot(n * (1 - 2 * i)))
            return carry

        lax.fori_loop(0, 2 if n < 4 else 1, one, 0)

    def odd(i):
        return 1 + 2 * (i // 2)

    events(0)
    prep_xs(1)
    prep_mate(0, 0)
    prep_loop(4, lambda i: (odd(i) * lax.rem(i, 2), odd(i) * (1 - lax.rem(i, 2))))
    for n in (1, 2, 3):
        ref = tabs.at[wrap4(x - n)]
        arrived(ref, l_recv.at[n - 1])
    tab_copy = pltpu.make_async_copy(tabs, tab_s, load_sem.at[1])
    tab_copy.start()
    tab_copy.wait()
    events(1)
    prep_xs(2)
    prep_loop(2, lambda i: (2 * i, 2 - 2 * i))
    pair_loop(5, lambda i: (x, z_slot(i - 2)))
    prep_loop(4, lambda i: (odd(i), 1 + 2 * lax.rem(i, 2)))
    events(2)
    prep_xs(3)
    prep_loop(4, lambda i: (odd(i) * lax.rem(i, 2) + 2 * (1 - lax.rem(i, 2)),
                            odd(i) * (1 - lax.rem(i, 2)) + 2 * lax.rem(i, 2)))
    pair_loop(2, lambda i: (x, z_slot(6 * i - 3)))
    pair_loop(7, lambda i: (wrap4(x - 1), z_slot(i - 3)))
    events(3)
    prep_xs(4)
    pair_loop(7, lambda i: (wrap4(x + 1), z_slot(i - 3)))
    pair_loop(3, lambda i: (wrap4(x - i - i // 2), z_slot(4)))
    prep_loop(1, lambda i: (2 + i, 2 + i))
    pair_loop(8, lambda i: (wrap4(x + 2), z_slot(i - 3)))

    def close(b, logs):
        high = jnp.max(top[b], axis=1, keepdims=True)
        whole = jnp.sum(total[b] * jnp.exp2(top[b] - high), axis=1, keepdims=True)
        mine_b = jnp.where(whole > 0.0, high + jnp.log2(whole), LOWEST)
        lane = lax.broadcasted_iota(jnp.int32, (BLK, 128), 1)
        return jnp.where(lane == b, mine_b, logs)

    logs = lax.fori_loop(0, NZ, close, jnp.zeros((BLK, 128), jnp.float32)).T[0:NZ]
    row_out[:, pl.ds(0, BLK)] = logs
    row_out[:, pl.ds(BLK, 128)] = jnp.broadcast_to(bad, (NZ, 128))
    for n in range(1, NZ):
        start(remote(row_out, row_got.at[n - 1], row_send.at[n - 1], row_recv.at[n - 1],
                     device(y, k, x, lax.rem(z + n, NZ))))
    own_x = x_raw[z, pl.ds(0, BLK), :]
    own_x = jnp.broadcast_to(jnp.sum(own_x * own_x, axis=1, keepdims=True), (BLK, 128)).T[0:1]
    own_y = y_raw[x, row, pl.ds(0, BLK), :]
    own_y = jnp.broadcast_to(jnp.sum(own_y * own_y, axis=1, keepdims=True), (BLK, 128)).T[0:1]
    masses = x_raw[:, pl.ds(BLK, 1), :].reshape(NZ, BLK)
    for n in range(1, NZ):
        arrived(row_got.at[n - 1], row_recv.at[n - 1])
    others = [row_got[n, :, pl.ds(0, BLK)] for n in range(NZ - 1)]
    for n in range(NZ - 1):
        bad = jnp.maximum(bad, row_got[n, pl.ds(0, 1), pl.ds(BLK, 128)])
    high = logs
    for v in others:
        high = jnp.maximum(high, v)
    whole = jnp.exp2(logs - high)
    for v in others:
        whole = whole + jnp.exp2(v - high)
    logs = high + jnp.log2(whole)
    shift = LOG2E * masses - logs
    row_logs[...] = logs
    f_out[...] = (ENTROPY * x_raw[z, pl.ds(BLK, 1), :] - (ENTROPY * LN2) * row_logs[pl.ds(z, 1), :]
                  + own_x * (1.0 / D))
    for b in range(NZ):
        top[b] = jnp.broadcast_to(shift[b:b + 1], (128, BLK)).T

    def second(i, carry):
        xq, zb = i // NZ, lax.rem(i, NZ)
        for n in (0, 1):
            for h in (0, 128):
                u = (scores[xq, n, zb, :, pl.ds(h, 128)] + top[zb]).reshape(BLK // 8, 8, 128)
                m = jnp.max(u, axis=0)
                col_top[xq, n, zb, :, pl.ds(h, 128)] = m
                col_sum[xq, n, zb, :, pl.ds(h, 128)] = jnp.sum(jnp.exp2(u - m[None]), axis=0)
        return carry

    lax.fori_loop(0, NX * NZ, second, 0)

    def columns(xq, carry):
        m = col_top[xq].reshape(2 * NZ, 8, BLK)
        high = jnp.max(m, axis=1)
        whole = jnp.sum(col_sum[xq].reshape(2 * NZ, 8, BLK) * jnp.exp2(m - high[:, None, :]), axis=1)
        slots = high + jnp.log2(whole)
        named = tabs[xq]
        named = jnp.concatenate([jnp.broadcast_to(named[:, 0:1], (NZ, BLK)),
                                 jnp.broadcast_to(named[:, 64:65], (NZ, BLK))], axis=0)
        for t in range(N_ROW):
            v = jnp.where(named == t + 1, slots, LOWEST)
            high = jnp.max(v, axis=0, keepdims=True)
            whole = jnp.sum(jnp.exp2(v - high), axis=0, keepdims=True)
            col_out[xq, t, :, pl.ds(0, BLK)] = high + jnp.log2(whole)
            col_out[xq, t, :, pl.ds(BLK, 128)] = bad
        return carry

    lax.fori_loop(0, NX, columns, 0)
    many = NX * N_ROW
    me = x * N_ROW + row

    def peer(n):
        other = lax.rem(me + n, many)
        return other // N_ROW, lax.rem(other, N_ROW)

    for n in range(1, many):
        ox, orow = peer(n)
        start(remote(col_out.at[ox, orow], col_got.at[n], col_send.at[n], col_recv.at[n],
                     {"row": orow, "col": ox * NZ + z}))
    col_got[0] = col_out[x, row]
    for n in range(1, many):
        arrived(col_got.at[n], col_recv.at[n])
    every = col_got[:, :, pl.ds(0, BLK)]
    high = jnp.max(every, axis=0)
    whole = jnp.sum(jnp.exp2(every - high[None]), axis=0)
    g_out[...] = (ENTROPY * mass_b_ref[...] - (ENTROPY * LN2) * (high + jnp.log2(whole)) + own_y * (1.0 / D))
    bad_out[...] = jnp.max(col_got[:, :, pl.ds(BLK, 128)], axis=0)
    for copy in pending:
        copy.wait_send()


def shape(*dims, kind=jnp.float32):
    return jax.ShapeDtypeStruct(dims, kind)


def general(sources, targets, g_pot, log_a, log_b, src_block, tgt_block, pair_count):
    whole = pl.BlockSpec(memory_space=pltpu.VMEM)
    anywhere = pl.BlockSpec(memory_space=pl.ANY)
    scalars = pl.BlockSpec(memory_space=pltpu.SMEM)
    dma = pltpu.SemaphoreType.DMA
    packed = jnp.zeros((8, 128), jnp.int32)
    packed = packed.at[0, :64].set(src_block).at[0, 64:].set(tgt_block).at[1, 0].set(pair_count[0])
    x_raw, y_raw, lists = pl.pallas_call(
        gather_kernel,
        out_shape=(shape(NZ, ROWS, D), shape(NX, N_ROW, ROWS, D), shape(NX, 8, 128, kind=jnp.int32)),
        in_specs=[anywhere] * 5,
        out_specs=(whole, whole, whole),
        scratch_shapes=[dma((5,)), dma((16, 2, 4)), dma((16, 2)), dma((16, 2)), dma((16, 2)),
                        dma((9, 2, 2)), dma((9, 2)), dma((3,)), dma((3,))],
        compiler_params=pltpu.CompilerParams(collective_id=3, has_side_effects=True, vmem_limit_bytes=VMEM_LIMIT),
    )(sources, targets, g_pot[None], log_a[None], packed)
    y_raw = y_raw.reshape(NX * N_ROW, ROWS, D)
    quarter = (lax.axis_index("col") // NZ).astype(jnp.int32).reshape(1)
    x3, y3, part = pl.pallas_call(
        first_kernel,
        out_shape=(shape(NZ, BLK, 3 * D, kind=jnp.bfloat16), shape(NX * N_ROW, 3 * D, BLK, kind=jnp.bfloat16),
                   shape(NZ, 8, BLK)),
        in_specs=[scalars, scalars, whole, whole],
        out_specs=(whole, whole, whole),
        scratch_shapes=[pltpu.VMEM((NX * N_ROW, 8, BLK), jnp.float32), pltpu.VMEM((NZ, BLK, 128), jnp.float32),
                        pltpu.VMEM((NZ, BLK, 128), jnp.float32)],
        compiler_params=pltpu.CompilerParams(vmem_limit_bytes=VMEM_LIMIT),
    )(lists, quarter, x_raw, y_raw)
    f_own, c_all = pl.pallas_call(
        row_exchange_kernel,
        out_shape=(shape(1, BLK), shape(NZ, 8, BLK)),
        in_specs=[whole, whole],
        out_specs=(whole, whole),
        scratch_shapes=[pltpu.VMEM((NZ - 1, NZ, 8, BLK), jnp.float32), dma((NZ - 1,)), dma((NZ - 1,))],
        compiler_params=pltpu.CompilerParams(collective_id=1, has_side_effects=True, vmem_limit_bytes=VMEM_LIMIT),
    )(part, x_raw)
    sums = pl.pallas_call(
        second_kernel,
        out_shape=shape(NX * N_ROW, 1, BLK),
        in_specs=[scalars, scalars, whole, whole, whole],
        out_specs=whole,
        scratch_shapes=[pltpu.VMEM((NZ, BLK, 128), jnp.float32), pltpu.VMEM((NX * N_ROW, 8, BLK), jnp.float32),
                        pltpu.VMEM((NX * N_ROW, 8, BLK), jnp.float32)],
        compiler_params=pltpu.CompilerParams(vmem_limit_bytes=VMEM_LIMIT),
    )(lists, quarter, x3, y3, c_all)
    g_own = pl.pallas_call(
        col_exchange_kernel,
        out_shape=shape(1, BLK),
        in_specs=[whole, whole, whole],
        out_specs=whole,
        scratch_shapes=[pltpu.VMEM((NX * N_ROW, 1, BLK), jnp.float32), dma((NX * N_ROW,)), dma((NX * N_ROW,))],
        compiler_params=pltpu.CompilerParams(collective_id=2, has_side_effects=True),
    )(sums, targets, log_b[None])
    return f_own.reshape(BLK), g_own.reshape(BLK)


def local(sources, targets, g_pot, log_a, log_b, src_block, tgt_block, pair_count):
    whole = pl.BlockSpec(memory_space=pltpu.VMEM)
    anywhere = pl.BlockSpec(memory_space=pl.ANY)
    scalars = pl.BlockSpec(memory_space=pltpu.SMEM)
    dma = pltpu.SemaphoreType.DMA
    vmem = pltpu.VMEM
    f32 = jnp.float32
    f_own, g_own, bad = pl.pallas_call(
        merged_kernel,
        out_shape=(shape(1, BLK), shape(1, BLK), shape(1, 128)),
        in_specs=[scalars] * 3 + [anywhere] * 4 + [whole],
        out_specs=(whole, whole, whole),
        scratch_shapes=[
            vmem((NX, N_ROW, ROWS, D), f32), vmem((NZ, ROWS, D), f32),
            vmem((NX, N_ROW, BLK, 3 * D), jnp.bfloat16), vmem((NZ, BLK, 3 * D), jnp.bfloat16),
            vmem((NX, N_ROW, 8, BLK), f32), vmem((NZ, BLK, 128), f32), vmem((NZ, BLK, 128), f32),
            vmem((NX, 2, NZ, BLK, BLK), f32), vmem((NX, 2, NZ, 8, BLK), f32), vmem((NX, 2, NZ, 8, BLK), f32),
            vmem((NX, NZ, 128), jnp.int32), pltpu.SMEM((NX, NZ, 128), jnp.int32), vmem((N_COL, 128), jnp.int32),
            vmem((NZ, BLK + 128), f32), vmem((NZ, BLK), f32), vmem((NZ - 1, NZ, BLK + 128), f32),
            vmem((NX, N_ROW, 1, BLK + 128), f32), vmem((NX * N_ROW, 1, BLK + 128), f32),
            dma((4,)), dma((16, 2, 4)), dma((16, 2)), dma((16, 2)), dma((16, 2)),
            dma((9, 2, 2)), dma((9, 2)), dma((3,)), dma((3,)),
            dma((NZ - 1,)), dma((NZ - 1,)), dma((NX * N_ROW,)), dma((NX * N_ROW,))],
        compiler_params=pltpu.CompilerParams(collective_id=0, has_side_effects=True, vmem_limit_bytes=VMEM_LIMIT),
    )(src_block, tgt_block, pair_count, sources, targets, g_pot[None], log_a[None], log_b[None])
    args = (sources, targets, g_pot, log_a, log_b, src_block, tgt_block, pair_count)
    return lax.cond(bad[0, 0] > 0.5, lambda: general(*args), lambda: (f_own.reshape(BLK), g_own.reshape(BLK)))


def solution(mesh):
    placed = (
        P(("row", "col"), None),
        P(("col", "row"), None),
        P(("col", "row")),
        P(("row", "col")),
        P(("col", "row")),
        P(("row", "col")),
        P(("row", "col")),
        P(("row", "col")),
    )
    return jax.shard_map(
        local,
        mesh=mesh,
        in_specs=placed,
        out_specs=(P(("row", "col")), P(("col", "row"))),
        check_vma=False,
    )
```

profile of v0, /device:TPU:1, one launch (start us, length us, event | category | flops | bytes accessed | tf_op | source)
XLA Modules:
  0.0 74.3 jit_solution(1417181337665440663)
XLA Ops:
  1.3 71.2 %shard_map.95 = (f32[1,256]{1,0:T(1,128)S(1)}, f32[1,256]{1,0:T(1,128)S(1)}, f32[1,128]{1,0:T(1,128)}) custom-call(s32[64]{0:T(128)} %src_list.1, s32[64]{0:T(128)} %tgt_list.1, s32[1]{0:T(128)S(6)} %copy.20.count_ref, f32[256,256]{1,0:T(8,128)} %src_ref.1, f32[256,256]{1,0:T(8,128)} %tgt_ref.1, f32[1,256]{1,0:T(1,128)} %bitcast.23, f32[1,256]{1,0:T(1,128)} %bitcast.25, ...), custom_call_target="tpu_custom_call" | custom-call | tf_op jit(solution)/shard_map/pallas_call | solution.py:771
  73.1 0.6 copy.21
  73.7 0.6 copy.22
  (1 shorter events, 0.0 us)
where the time goes:
time: 74.4 us; the launch traced here: 74.3 us
  Pallas kernels  71.2 us (96%)
  between operations  1.97 us (3%)
  local copies, waits for them, and re-layouts  1.13 us (2%)
    pallas_call x1, Pallas kernels, local(): pl.pallas_call(merged_kernel, out_shape=(shape(1, BLK), shape(1, BLK), sh...  71.2 us

commit v1 on v0

--- a/solution.py
+++ b/solution.py
@@ -55,6 +55,37 @@
     elif db == 3 and da in (2, 3):
         out += [("B-", (da, 2))]
     return out
+
+
+REACHED = FIRST + SECOND + THIRD + FOURTH
+OTHER_WAY = {"A+": "A-", "A-": "A+", "B+": "B+", "B-": "B-"}
+
+
+def mirror(pos):
+    return (4 - pos[0]) % 4, pos[1]
+
+
+def chunk_sends(pos, ch):
+    if ch == 0:
+        return sends_of(*pos)
+    return [(OTHER_WAY[name], mirror(target)) for name, target in sends_of(*mirror(pos))]
+
+
+PARTS = ((0, 128), (128, 136))
+STEPS = (
+    ("X", 0), ("Y", 0, 0), ("M", 0, 0), ("y", 0, 3, 0), ("z", -1, 0), ("y", 3, 0, 0), ("y", 1, 0, 0), ("z", 1, 0),
+    ("y", 0, 1, 0), ("y", 1, 0, 1), ("y", 0, 1, 1), ("z", 1, 1), ("y", 0, 3, 1), ("z", -1, 1), ("y", 3, 0, 1),
+    ("X", 1), ("X", -1), ("Y", 1, 0), ("Y", 3, 0), ("Y", 0, 1), ("Y", 0, 3), ("M", 1, 0), ("M", 0, 1), ("M", 0, 3),
+    ("z", -2, 0), ("z", 2, 0), ("y", 3, 1, 0), ("y", 3, 3, 0), ("y", 2, 0, 0), ("M", 3, 0), ("y", 2, 0, 1),
+    ("Y", 2, 0), ("y", 1, 3, 0), ("y", 1, 1, 0), ("M", 2, 0), ("y", 0, 2, 0), ("z", -2, 1), ("z", 2, 1), ("X", 2),
+    ("y", 1, 3, 1), ("X", -2), ("Y", 1, 3), ("y", 1, 1, 1), ("Y", 1, 1), ("y", 3, 3, 1), ("Y", 3, 3), ("M", 1, 3),
+    ("z", -3, 0), ("z", 3, 0), ("M", 1, 1), ("y", 0, 2, 1), ("y", 3, 2, 0), ("Y", 0, 2), ("M", 3, 3), ("y", 2, 3, 0),
+    ("M", 0, 2), ("y", 3, 1, 1), ("Y", 3, 1), ("D", 0, 1), ("y", 2, 1, 0), ("z", -3, 1), ("y", 2, 3, 1), ("z", 3, 1),
+    ("X", 3), ("X", -3), ("Y", 2, 3), ("M", 3, 1), ("D", -1, 2), ("z", 4, 0), ("y", 1, 2, 1), ("y", 2, 1, 1),
+    ("Y", 2, 1), ("D", -2, 3), ("M", 2, 3), ("z", 4, 1), ("y", 1, 2, 0), ("y", 2, 2, 0), ("X", 4), ("Y", 1, 2),
+    ("D", -3, 4), ("M", 2, 1), ("M", 1, 2), ("y", 3, 2, 1), ("y", 2, 2, 1), ("Y", 3, 2), ("Y", 2, 2), ("M", 3, 2),
+    ("M", 2, 2),
+)
 
 
 def gather_kernel(src_ref, tgt_ref, pot_ref, mass_ref, list_ref, x_out, y_out, lists_out,
@@ -423,26 +454,6 @@
     for peer in peers:
         signal(barrier, peer)
 
-    ids = lax.broadcasted_iota(jnp.int32, (N_COL, 128), 0)
-    left = lax.broadcasted_iota(jnp.int32, (N_COL, 128), 1) < 64
-    live = count_ref[0]
-
-    def enter(i, carry):
-        table, named = carry
-        one = jnp.where(i < live, tgt_list[i] + 1, 0)
-        two = jnp.where(i + 32 < live, tgt_list[i + 32] + 1, 0)
-        here = ids == src_list[i]
-        table = table + jnp.where(here, jnp.where(left, one, two), 0)
-        named = named + jnp.where(here, jnp.where(i < live, 1, 0), 0)
-        return table, named
-
-    nothing = jnp.zeros((N_COL, 128), jnp.int32)
-    table, named = lax.fori_loop(0, 32, enter, (nothing, nothing))
-    mine[...] = jnp.minimum(table, N_ROW)
-    bad = jnp.max(jnp.where(named > 1, 1.0, 0.0), axis=0, keepdims=True)
-    top[...] = jnp.full(top.shape, LOWEST, jnp.float32)
-    total[...] = jnp.zeros(total.shape, jnp.float32)
-
     pl.semaphore_wait(barrier, len(peers))
     for copy in loads:
         copy.wait()
@@ -453,7 +464,7 @@
         return pos[0] * 4 + pos[1]
 
     def part(ref, ch):
-        return ref.at[pl.ds(*CHUNKS[ch])]
+        return ref.at[pl.ds(*PARTS[ch])]
 
     def remote(src, dst, send, recv, where):
         return pltpu.make_async_remote_copy(src_ref=src, dst_ref=dst, send_sem=send, recv_sem=recv,
@@ -468,7 +479,7 @@
 
     def send_y(pos, ch):
         ref = part(y_raw.at[slot(*pos, k)], ch)
-        for n, (name, target) in enumerate(sends_of(*pos)):
+        for n, (name, target) in enumerate(chunk_sends(pos, ch)):
             start(remote(ref, ref, send_sem.at[at(pos), ch, n], recv_sem.at[at(target), ch], dev_of(name)))
 
     def send_mate(pos, ch):
@@ -511,15 +522,6 @@
         for ch in (0, 1):
             arrived(part(y_raw.at[slot(da, db, 1 - k)], ch), mate_recv.at[da * 4 + db, ch])
         prep_y(da, db, 1 - k)
-
-    def prep_loop(many, pos):
-        def one(i, carry):
-            da, db = pos(i)
-            prep_y(da, db, k)
-            prep_mate(da, db)
-            return carry
-
-        lax.fori_loop(0, many, one, 0)
 
     def pair(xq, zb):
         parts = []
@@ -537,131 +539,144 @@
         total[zb] = total[zb] * jnp.exp2(old - new) + ((e[0] + e[1]) + (e[2] + e[3]))
         top[zb] = new
 
-    def pair_loop(many, which):
-        def one(i, carry):
-            pair(*which(i))
-            return carry
-
-        lax.fori_loop(0, many, one, 0)
-
     for ch in (0, 1):
         send_y((0, 0), ch)
         send_z(0, ch, True)
         send_z(0, ch, False)
         send_mate((0, 0), ch)
+    ids = lax.broadcasted_iota(jnp.int32, (N_COL, 128), 0)
+    left = lax.broadcasted_iota(jnp.int32, (N_COL, 128), 1) < 64
+    live = count_ref[0]
+
+    def enter(i, carry):
+        table, named = carry
+        one = jnp.where(i < live, tgt_list[i] + 1, 0)
+        two = jnp.where(i + 32 < live, tgt_list[i + 32] + 1, 0)
+        here = ids == src_list[i]
+        table = table + jnp.where(here, jnp.where(left, one, two), 0)
+        named = named + jnp.where(here, jnp.where(i < live, 1, 0), 0)
+        return table, named
+
+    nothing = jnp.zeros((N_COL, 128), jnp.int32)
+    table, named = lax.fori_loop(0, 32, enter, (nothing, nothing))
+    mine[...] = jnp.minimum(table, N_ROW)
+    bad = jnp.max(jnp.where(named > 1, 1.0, 0.0), axis=0, keepdims=True)
+    top[...] = jnp.full(top.shape, LOWEST, jnp.float32)
+    total[...] = jnp.zeros(total.shape, jnp.float32)
+
     keep = pltpu.make_async_copy(mine.at[pl.ds(x * NZ, NZ)], tabs.at[x], load_sem.at[0])
     keep.start()
     for n in (1, 2, 3):
         to = wrap4(x + n)
         start(remote(mine.at[pl.ds(to * NZ, NZ)], tabs.at[x], l_send.at[n - 1], l_recv.at[n - 1], device(y, k, to, z)))
     keep.wait()
-    prep_x(z)
-    prep_y(0, 0, k)
-
-    levels = (FIRST, SECOND, THIRD, FOURTH)
-
-    def events(level):
-        n = level + 1
-        for ch in (0, 1):
-            for pos in levels[level]:
-                recv_y(pos, ch)
-                send_y(pos, ch)
-                send_mate(pos, ch)
+    tab_copy = pltpu.make_async_copy(tabs, tab_s, load_sem.at[1])
+    paired = 0
+    for step in STEPS:
+        kind = step[0]
+        if kind == "y":
+            pos, ch = step[1:3], step[3]
+            recv_y(pos, ch)
+            send_y(pos, ch)
+            send_mate(pos, ch)
+        elif kind == "z":
+            n, ch = step[1:]
             recv_z(n, ch)
-            if n < 4:
+            if 0 < n < 4:
                 send_z(n, ch, True)
-                recv_z(-n, ch)
-                if n < 3:
-                    send_z(-n, ch, False)
-
-    def prep_xs(n):
-        def one(i, carry):
-            prep_x(z_slot(n * (1 - 2 * i)))
-            return carry
-
-        lax.fori_loop(0, 2 if n < 4 else 1, one, 0)
-
-    def odd(i):
-        return 1 + 2 * (i // 2)
-
-    events(0)
-    prep_xs(1)
-    prep_mate(0, 0)
-    prep_loop(4, lambda i: (odd(i) * lax.rem(i, 2), odd(i) * (1 - lax.rem(i, 2))))
-    for n in (1, 2, 3):
-        ref = tabs.at[wrap4(x - n)]
-        arrived(ref, l_recv.at[n - 1])
-    tab_copy = pltpu.make_async_copy(tabs, tab_s, load_sem.at[1])
-    tab_copy.start()
-    tab_copy.wait()
-    events(1)
-    prep_xs(2)
-    prep_loop(2, lambda i: (2 * i, 2 - 2 * i))
-    pair_loop(5, lambda i: (x, z_slot(i - 2)))
-    prep_loop(4, lambda i: (odd(i), 1 + 2 * lax.rem(i, 2)))
-    events(2)
-    prep_xs(3)
-    prep_loop(4, lambda i: (odd(i) * lax.rem(i, 2) + 2 * (1 - lax.rem(i, 2)),
-                            odd(i) * (1 - lax.rem(i, 2)) + 2 * lax.rem(i, 2)))
-    pair_loop(2, lambda i: (x, z_slot(6 * i - 3)))
-    pair_loop(7, lambda i: (wrap4(x - 1), z_slot(i - 3)))
-    events(3)
-    prep_xs(4)
-    pair_loop(7, lambda i: (wrap4(x + 1), z_slot(i - 3)))
-    pair_loop(3, lambda i: (wrap4(x - i - i // 2), z_slot(4)))
-    prep_loop(1, lambda i: (2 + i, 2 + i))
-    pair_loop(8, lambda i: (wrap4(x + 2), z_slot(i - 3)))
-
-    def close(b, logs):
+            if -3 < n < 0:
+                send_z(n, ch, False)
+        elif kind == "X":
+            prep_x(z_slot(step[1]))
+            if step[1] == -1:
+                for n in (1, 2, 3):
+                    arrived(tabs.at[wrap4(x - n)], l_recv.at[n - 1])
+                tab_copy.start()
+        elif kind == "Y":
+            prep_y(step[1], step[2], k)
+        elif kind == "M":
+            prep_mate(step[1], step[2])
+        else:
+            if not paired:
+                tab_copy.wait()
+            paired += 1
+            pair(x, z_slot(step[1]))
+            pair(x, z_slot(step[2]))
+
+    def sides(i, carry):
+        xq = wrap4(x + 1 + 2 * (i // 4))
+        zb = 2 * lax.rem(i, 4)
+        pair(xq, zb)
+        pair(xq, zb + 1)
+        return carry
+
+    lax.fori_loop(0, 8, sides, 0)
+
+    def row_copy(b, n):
+        return remote(row_out.at[b], row_got.at[b, n - 1], row_send.at[b, n - 1], row_recv.at[b, n - 1],
+                      device(y, k, x, lax.rem(z + n, NZ)))
+
+    def close(b):
         high = jnp.max(top[b], axis=1, keepdims=True)
         whole = jnp.sum(total[b] * jnp.exp2(top[b] - high), axis=1, keepdims=True)
-        mine_b = jnp.where(whole > 0.0, high + jnp.log2(whole), LOWEST)
-        lane = lax.broadcasted_iota(jnp.int32, (BLK, 128), 1)
-        return jnp.where(lane == b, mine_b, logs)
-
-    logs = lax.fori_loop(0, NZ, close, jnp.zeros((BLK, 128), jnp.float32)).T[0:NZ]
-    row_out[:, pl.ds(0, BLK)] = logs
-    row_out[:, pl.ds(BLK, 128)] = jnp.broadcast_to(bad, (NZ, 128))
-    for n in range(1, NZ):
-        start(remote(row_out, row_got.at[n - 1], row_send.at[n - 1], row_recv.at[n - 1],
-                     device(y, k, x, lax.rem(z + n, NZ))))
-    own_x = x_raw[z, pl.ds(0, BLK), :]
-    own_x = jnp.broadcast_to(jnp.sum(own_x * own_x, axis=1, keepdims=True), (BLK, 128)).T[0:1]
-    own_y = y_raw[x, row, pl.ds(0, BLK), :]
-    own_y = jnp.broadcast_to(jnp.sum(own_y * own_y, axis=1, keepdims=True), (BLK, 128)).T[0:1]
-    masses = x_raw[:, pl.ds(BLK, 1), :].reshape(NZ, BLK)
-    for n in range(1, NZ):
-        arrived(row_got.at[n - 1], row_recv.at[n - 1])
-    others = [row_got[n, :, pl.ds(0, BLK)] for n in range(NZ - 1)]
-    for n in range(NZ - 1):
-        bad = jnp.maximum(bad, row_got[n, pl.ds(0, 1), pl.ds(BLK, 128)])
-    high = logs
-    for v in others:
-        high = jnp.maximum(high, v)
-    whole = jnp.exp2(logs - high)
-    for v in others:
-        whole = whole + jnp.exp2(v - high)
-    logs = high + jnp.log2(whole)
-    shift = LOG2E * masses - logs
-    row_logs[...] = logs
-    f_out[...] = (ENTROPY * x_raw[z, pl.ds(BLK, 1), :] - (ENTROPY * LN2) * row_logs[pl.ds(z, 1), :]
-                  + own_x * (1.0 / D))
-    for b in range(NZ):
-        top[b] = jnp.broadcast_to(shift[b:b + 1], (128, BLK)).T
-
-    def second(i, carry):
-        xq, zb = i // NZ, lax.rem(i, NZ)
+        logs = jnp.where(whole > 0.0, high + jnp.log2(whole), LOWEST)
+        row_out[b, :, pl.ds(0, BLK)] = jnp.broadcast_to(logs, (BLK, 128)).T[0:1]
+        row_out[b, :, pl.ds(BLK, 128)] = bad
+
+    def far(i, carry):
+        for b in (2 * i, 2 * i + 1):
+            pair(wrap4(x + 2), b)
+        for b in (2 * i, 2 * i + 1):
+            close(b)
+        for b in (2 * i, 2 * i + 1):
+            for n in range(1, NZ):
+                row_copy(b, n).start()
+        return carry
+
+    lax.fori_loop(0, NZ // 2, far, 0)
+
+    def rows_of(b, bad):
+        for n in range(1, NZ):
+            arrived(row_got.at[b, n - 1], row_recv.at[b, n - 1])
+        own = row_out[b, :, pl.ds(0, BLK)]
+        others = [row_got[b, n, :, pl.ds(0, BLK)] for n in range(NZ - 1)]
+        for n in range(NZ - 1):
+            bad = jnp.maximum(bad, row_got[b, n, :, pl.ds(BLK, 128)])
+        high = own
+        for v in others:
+            high = jnp.maximum(high, v)
+        whole = jnp.exp2(own - high)
+        for v in others:
+            whole = whole + jnp.exp2(v - high)
+        logs = high + jnp.log2(whole)
+        row_logs[pl.ds(b, 1), :] = logs
+        shift = LOG2E * x_raw[b, pl.ds(BLK, 1), :] - logs
+        top[b] = jnp.broadcast_to(shift, (128, BLK)).T
+        return bad
+
+    def second(xq, zb):
         for n in (0, 1):
             for h in (0, 128):
                 u = (scores[xq, n, zb, :, pl.ds(h, 128)] + top[zb]).reshape(BLK // 8, 8, 128)
                 m = jnp.max(u, axis=0)
                 col_top[xq, n, zb, :, pl.ds(h, 128)] = m
                 col_sum[xq, n, zb, :, pl.ds(h, 128)] = jnp.sum(jnp.exp2(u - m[None]), axis=0)
-        return carry
-
-    lax.fori_loop(0, NX * NZ, second, 0)
-
-    def columns(xq, carry):
+
+    def early(b, bad):
+        bad = rows_of(b, bad)
+
+        def one(i, carry):
+            second(2 * i, b)
+            second(2 * i + 1, b)
+            return carry
+
+        lax.fori_loop(0, NX // 2, one, 0)
+        return bad
+
+    bad = lax.fori_loop(0, NZ - 2, early, bad)
+    bad = rows_of(NZ - 1, rows_of(NZ - 2, bad))
+
+    def columns(xq):
         m = col_top[xq].reshape(2 * NZ, 8, BLK)
         high = jnp.max(m, axis=1)
         whole = jnp.sum(col_sum[xq].reshape(2 * NZ, 8, BLK) * jnp.exp2(m - high[:, None, :]), axis=1)
@@ -675,28 +690,43 @@
             whole = jnp.sum(jnp.exp2(v - high), axis=0, keepdims=True)
             col_out[xq, t, :, pl.ds(0, BLK)] = high + jnp.log2(whole)
             col_out[xq, t, :, pl.ds(BLK, 128)] = bad
+
+    def col_copy(xq, t):
+        return remote(col_out.at[xq, t], col_got.at[x, row], col_send.at[xq, t], col_recv.at[x, row],
+                      {"row": t, "col": xq * NZ + z})
+
+    for away in (2, 1, 3, 0):
+        xq = wrap4(x + away)
+        second(xq, NZ - 2)
+        second(xq, NZ - 1)
+        columns(xq)
+        for n in range(N_ROW):
+            if away or n:
+                start(col_copy(xq, lax.rem(row + n, N_ROW)))
+    f_square = x_raw[z, pl.ds(0, BLK), :]
+    f_square = jnp.broadcast_to(jnp.sum(f_square * f_square, axis=1, keepdims=True), (BLK, 128)).T[0:1]
+    g_square = y_raw[x, row, pl.ds(0, BLK), :]
+    g_square = jnp.broadcast_to(jnp.sum(g_square * g_square, axis=1, keepdims=True), (BLK, 128)).T[0:1]
+    f_out[...] = (ENTROPY * x_raw[z, pl.ds(BLK, 1), :] - (ENTROPY * LN2) * row_logs[pl.ds(z, 1), :]
+                  + f_square * (1.0 / D))
+    col_got[x, row] = col_out[x, row]
+    for away in (2, 1, 3, 0):
+        for n in range(N_ROW):
+            if away or n:
+                ox, orow = wrap4(x + away), lax.rem(row + n, N_ROW)
+                arrived(col_got.at[ox, orow], col_recv.at[ox, orow])
+    every = col_got[...].reshape(NX * N_ROW, 1, BLK + 128)
+    high = jnp.max(every[:, :, :BLK], axis=0)
+    whole = jnp.sum(jnp.exp2(every[:, :, :BLK] - high[None]), axis=0)
+    g_out[...] = (ENTROPY * mass_b_ref[...] - (ENTROPY * LN2) * (high + jnp.log2(whole)) + g_square * (1.0 / D))
+    bad_out[...] = jnp.max(every[:, :, BLK:], axis=0)
+
+    def sent(b, carry):
+        for n in range(1, NZ):
+            row_copy(b, n).wait_send()
         return carry
 
-    lax.fori_loop(0, NX, columns, 0)
-    many = NX * N_ROW
-    me = x * N_ROW + row
-
-    def peer(n):
-        other = lax.rem(me + n, many)
-        return other // N_ROW, lax.rem(other, N_ROW)
-
-    for n in range(1, many):
-        ox, orow = peer(n)
-        start(remote(col_out.at[ox, orow], col_got.at[n], col_send.at[n], col_recv.at[n],
-                     {"row": orow, "col": ox * NZ + z}))
-    col_got[0] = col_out[x, row]
-    for n in range(1, many):
-        arrived(col_got.at[n], col_recv.at[n])
-    every = col_got[:, :, pl.ds(0, BLK)]
-    high = jnp.max(every, axis=0)
-    whole = jnp.sum(jnp.exp2(every - high[None]), axis=0)
-    g_out[...] = (ENTROPY * mass_b_ref[...] - (ENTROPY * LN2) * (high + jnp.log2(whole)) + own_y * (1.0 / D))
-    bad_out[...] = jnp.max(col_got[:, :, pl.ds(BLK, 128)], axis=0)
+    lax.fori_loop(0, NZ, sent, 0)
     for copy in pending:
         copy.wait_send()
 
@@ -779,11 +809,11 @@
             vmem((NX, N_ROW, 8, BLK), f32), vmem((NZ, BLK, 128), f32), vmem((NZ, BLK, 128), f32),
             vmem((NX, 2, NZ, BLK, BLK), f32), vmem((NX, 2, NZ, 8, BLK), f32), vmem((NX, 2, NZ, 8, BLK), f32),
             vmem((NX, NZ, 128), jnp.int32), pltpu.SMEM((NX, NZ, 128), jnp.int32), vmem((N_COL, 128), jnp.int32),
-            vmem((NZ, BLK + 128), f32), vmem((NZ, BLK), f32), vmem((NZ - 1, NZ, BLK + 128), f32),
-            vmem((NX, N_ROW, 1, BLK + 128), f32), vmem((NX * N_ROW, 1, BLK + 128), f32),
+            vmem((NZ, 1, BLK + 128), f32), vmem((NZ, BLK), f32), vmem((NZ, NZ - 1, 1, BLK + 128), f32),
+            vmem((NX, N_ROW, 1, BLK + 128), f32), vmem((NX, N_ROW, 1, BLK + 128), f32),
             dma((4,)), dma((16, 2, 4)), dma((16, 2)), dma((16, 2)), dma((16, 2)),
             dma((9, 2, 2)), dma((9, 2)), dma((3,)), dma((3,)),
-            dma((NZ - 1,)), dma((NZ - 1,)), dma((NX * N_ROW,)), dma((NX * N_ROW,))],
+            dma((NZ, NZ - 1)), dma((NZ, NZ - 1)), dma((NX, N_ROW)), dma((NX, N_ROW))],
         compiler_params=pltpu.CompilerParams(collective_id=0, has_side_effects=True, vmem_limit_bytes=VMEM_LIMIT),
     )(src_block, tgt_block, pair_count, sources, targets, g_pot[None], log_a[None], log_b[None])
     args = (sources, targets, g_pot, log_a, log_b, src_block, tgt_block, pair_count)

time: 74.4 us -> 67.2 us (0.903)
  Pallas kernels: 71.2 us -> 63.7 us
    pallas_call x1, Pallas kernels: 71.2 us -> 63.7 us  [local(): pl.pallas_call(merged_kernel, out_shape=(shape(1, BLK), shape(1, BLK), sh...]
where the time goes in v1:
time: 67.2 us; the launch traced here: 67.1 us
  Pallas kernels  63.7 us (95%)
  between operations  1.97 us (3%)
  local copies, waits for them, and re-layouts  1.13 us (2%)
    pallas_call x1, Pallas kernels, local(): pl.pallas_call(merged_kernel, out_shape=(shape(1, BLK), shape(1, BLK), sh...  63.7 us

profile of v1, /device:TPU:1, one launch (start us, length us, event | category | flops | bytes accessed | tf_op | source)
XLA Modules:
  0.0 67.1 jit_solution(8214078648354619487)
XLA Ops:
  1.3 63.7 %shard_map.95 = (f32[1,256]{1,0:T(1,128)S(1)}, f32[1,256]{1,0:T(1,128)S(1)}, f32[1,128]{1,0:T(1,128)}) custom-call(s32[64]{0:T(128)} %src_list.1, s32[64]{0:T(128)} %tgt_list.1, s32[1]{0:T(128)S(6)} %copy.20.count_ref, f32[256,256]{1,0:T(8,128)} %src_ref.1, f32[256,256]{1,0:T(8,128)} %tgt_ref.1, f32[1,256]{1,0:T(1,128)} %bitcast.23, f32[1,256]{1,0:T(1,128)} %bitcast.25, ...), custom_call_target="tpu_custom_call" | custom-call | tf_op jit(solution)/shard_map/pallas_call | solution.py:801
  65.7 0.2 conditional.1
  65.9 0.6 copy.21
  66.5 0.6 copy.22

commit v2 on v1

--- a/solution.py
+++ b/solution.py
@@ -73,18 +73,17 @@
 
 PARTS = ((0, 128), (128, 136))
 STEPS = (
-    ("X", 0), ("Y", 0, 0), ("M", 0, 0), ("y", 0, 3, 0), ("z", -1, 0), ("y", 3, 0, 0), ("y", 1, 0, 0), ("z", 1, 0),
-    ("y", 0, 1, 0), ("y", 1, 0, 1), ("y", 0, 1, 1), ("z", 1, 1), ("y", 0, 3, 1), ("z", -1, 1), ("y", 3, 0, 1),
-    ("X", 1), ("X", -1), ("Y", 1, 0), ("Y", 3, 0), ("Y", 0, 1), ("Y", 0, 3), ("M", 1, 0), ("M", 0, 1), ("M", 0, 3),
-    ("z", -2, 0), ("z", 2, 0), ("y", 3, 1, 0), ("y", 3, 3, 0), ("y", 2, 0, 0), ("M", 3, 0), ("y", 2, 0, 1),
-    ("Y", 2, 0), ("y", 1, 3, 0), ("y", 1, 1, 0), ("M", 2, 0), ("y", 0, 2, 0), ("z", -2, 1), ("z", 2, 1), ("X", 2),
-    ("y", 1, 3, 1), ("X", -2), ("Y", 1, 3), ("y", 1, 1, 1), ("Y", 1, 1), ("y", 3, 3, 1), ("Y", 3, 3), ("M", 1, 3),
-    ("z", -3, 0), ("z", 3, 0), ("M", 1, 1), ("y", 0, 2, 1), ("y", 3, 2, 0), ("Y", 0, 2), ("M", 3, 3), ("y", 2, 3, 0),
-    ("M", 0, 2), ("y", 3, 1, 1), ("Y", 3, 1), ("D", 0, 1), ("y", 2, 1, 0), ("z", -3, 1), ("y", 2, 3, 1), ("z", 3, 1),
-    ("X", 3), ("X", -3), ("Y", 2, 3), ("M", 3, 1), ("D", -1, 2), ("z", 4, 0), ("y", 1, 2, 1), ("y", 2, 1, 1),
-    ("Y", 2, 1), ("D", -2, 3), ("M", 2, 3), ("z", 4, 1), ("y", 1, 2, 0), ("y", 2, 2, 0), ("X", 4), ("Y", 1, 2),
-    ("D", -3, 4), ("M", 2, 1), ("M", 1, 2), ("y", 3, 2, 1), ("y", 2, 2, 1), ("Y", 3, 2), ("Y", 2, 2), ("M", 3, 2),
-    ("M", 2, 2),
+    ("X", 0), ("Y", 0, 0), ("M", 0, 0), ("y", 1, 0, 0), ("y", 0, 1, 0), ("z", 1, 0), ("y", 0, 3, 0), ("y", 3, 0, 0),
+    ("z", -1, 0), ("y", 1, 0, 1), ("y", 0, 1, 1), ("z", 1, 1), ("y", 0, 3, 1), ("y", 3, 0, 1), ("z", -1, 1), ("X", 1),
+    ("X", -1), ("Y", 1, 0), ("Y", 3, 0), ("Y", 0, 1), ("Y", 0, 3), ("M", 1, 0), ("M", 0, 1), ("M", 0, 3), ("z", 2, 0),
+    ("y", 2, 0, 0), ("y", 1, 3, 0), ("y", 1, 1, 0), ("z", -2, 0), ("M", 3, 0), ("y", 2, 0, 1), ("Y", 2, 0),
+    ("y", 3, 3, 0), ("y", 0, 2, 0), ("M", 2, 0), ("y", 3, 1, 0), ("z", -2, 1), ("z", 2, 1), ("X", 2), ("y", 1, 3, 1),
+    ("X", -2), ("Y", 1, 3), ("y", 1, 1, 1), ("Y", 1, 1), ("y", 3, 3, 1), ("Y", 3, 3), ("M", 1, 3), ("z", -3, 0),
+    ("z", 3, 0), ("M", 1, 1), ("y", 0, 2, 1), ("y", 2, 3, 0), ("Y", 0, 2), ("M", 3, 3), ("M", 0, 2), ("y", 2, 3, 1),
+    ("y", 3, 1, 1), ("Y", 3, 1), ("Y", 2, 3), ("D", 0, 1), ("z", -3, 1), ("z", 3, 1), ("y", 3, 2, 0), ("y", 2, 1, 0),
+    ("X", 3), ("X", -3), ("M", 2, 3), ("M", 3, 1), ("D", -1, 2), ("z", 4, 0), ("y", 1, 2, 0), ("y", 1, 2, 1),
+    ("Y", 1, 2), ("D", -2, 3), ("y", 2, 2, 0), ("y", 2, 1, 1), ("Y", 2, 1), ("z", 4, 1), ("X", 4), ("D", -3, 4),
+    ("M", 1, 2), ("y", 3, 2, 1), ("y", 2, 2, 1), ("Y", 3, 2), ("Y", 2, 2), ("M", 2, 1), ("M", 3, 2), ("M", 2, 2),
 )
 
 
@@ -407,9 +406,9 @@
     return lax.dot_general(a, b, (((1,), (1,)), ((), ())), preferred_element_type=jnp.float32)
 
 
-def merged_kernel(src_list, tgt_list, count_ref, src_ref, tgt_ref, pot_ref, mass_ref, mass_b_ref,
+def merged_kernel(src_in, tgt_in, count_in, src_ref, tgt_ref, pot_ref, mass_ref, mass_b_in,
                   f_out, g_out, bad_out,
-                  y_raw, x_raw, y3, x3, bias, top, total, scores, col_top, col_sum, tabs, tab_s, mine, row_out, row_logs, row_got,
+                  y_raw, x_raw, y3, x3, bias, top, total, scores, col_top, col_sum, tabs, tab_s, mine, src_list, tgt_list, count_ref, mass_b_ref, row_out, row_logs, row_got,
                   col_out, col_got,
                   load_sem, send_sem, recv_sem, mate_send, mate_recv, z_send, z_recv, l_send, l_recv,
                   row_send, row_recv, col_send, col_recv):
@@ -446,7 +445,13 @@
         pltpu.make_async_copy(src_ref, x_raw.at[z, pl.ds(0, BLK)], load_sem.at[2]),
         pltpu.make_async_copy(mass_ref, x_raw.at[z, pl.ds(BLK, 1)], load_sem.at[3]),
     ]
-    for copy in loads:
+    small = [
+        pltpu.make_async_copy(src_in, src_list, load_sem.at[4]),
+        pltpu.make_async_copy(tgt_in, tgt_list, load_sem.at[5]),
+        pltpu.make_async_copy(count_in, count_ref, load_sem.at[6]),
+        pltpu.make_async_copy(mass_b_in, mass_b_ref, load_sem.at[7]),
+    ]
+    for copy in loads + small:
         copy.start()
     barrier = pltpu.get_barrier_semaphore()
     peers = [device(y, k, wrap4(x + 1), z), device(y, k, wrap4(x + 3), z), device(y, k, wrap4(x + 2), z),
@@ -544,6 +549,8 @@
         send_z(0, ch, True)
         send_z(0, ch, False)
         send_mate((0, 0), ch)
+    for copy in small:
+        copy.wait()
     ids = lax.broadcasted_iota(jnp.int32, (N_COL, 128), 0)
     left = lax.broadcasted_iota(jnp.int32, (N_COL, 128), 1) < 64
     live = count_ref[0]
@@ -603,15 +610,6 @@
             pair(x, z_slot(step[1]))
             pair(x, z_slot(step[2]))
 
-    def sides(i, carry):
-        xq = wrap4(x + 1 + 2 * (i // 4))
-        zb = 2 * lax.rem(i, 4)
-        pair(xq, zb)
-        pair(xq, zb + 1)
-        return carry
-
-    lax.fori_loop(0, 8, sides, 0)
-
     def row_copy(b, n):
         return remote(row_out.at[b], row_got.at[b, n - 1], row_send.at[b, n - 1], row_recv.at[b, n - 1],
                       device(y, k, x, lax.rem(z + n, NZ)))
@@ -624,8 +622,9 @@
         row_out[b, :, pl.ds(BLK, 128)] = bad
 
     def far(i, carry):
-        for b in (2 * i, 2 * i + 1):
-            pair(wrap4(x + 2), b)
+        for away in (1, 3, 2):
+            for b in (2 * i, 2 * i + 1):
+                pair(wrap4(x + away), b)
         for b in (2 * i, 2 * i + 1):
             close(b)
         for b in (2 * i, 2 * i + 1):
@@ -794,14 +793,13 @@
 def local(sources, targets, g_pot, log_a, log_b, src_block, tgt_block, pair_count):
     whole = pl.BlockSpec(memory_space=pltpu.VMEM)
     anywhere = pl.BlockSpec(memory_space=pl.ANY)
-    scalars = pl.BlockSpec(memory_space=pltpu.SMEM)
     dma = pltpu.SemaphoreType.DMA
     vmem = pltpu.VMEM
     f32 = jnp.float32
     f_own, g_own, bad = pl.pallas_call(
         merged_kernel,
         out_shape=(shape(1, BLK), shape(1, BLK), shape(1, 128)),
-        in_specs=[scalars] * 3 + [anywhere] * 4 + [whole],
+        in_specs=[anywhere] * 8,
         out_specs=(whole, whole, whole),
         scratch_shapes=[
             vmem((NX, N_ROW, ROWS, D), f32), vmem((NZ, ROWS, D), f32),
@@ -809,9 +807,10 @@
             vmem((NX, N_ROW, 8, BLK), f32), vmem((NZ, BLK, 128), f32), vmem((NZ, BLK, 128), f32),
             vmem((NX, 2, NZ, BLK, BLK), f32), vmem((NX, 2, NZ, 8, BLK), f32), vmem((NX, 2, NZ, 8, BLK), f32),
             vmem((NX, NZ, 128), jnp.int32), pltpu.SMEM((NX, NZ, 128), jnp.int32), vmem((N_COL, 128), jnp.int32),
+            pltpu.SMEM((64,), jnp.int32), pltpu.SMEM((64,), jnp.int32), pltpu.SMEM((1,), jnp.int32), vmem((1, BLK), f32),
             vmem((NZ, 1, BLK + 128), f32), vmem((NZ, BLK), f32), vmem((NZ, NZ - 1, 1, BLK + 128), f32),
             vmem((NX, N_ROW, 1, BLK + 128), f32), vmem((NX, N_ROW, 1, BLK + 128), f32),
-            dma((4,)), dma((16, 2, 4)), dma((16, 2)), dma((16, 2)), dma((16, 2)),
+            dma((8,)), dma((16, 2, 4)), dma((16, 2)), dma((16, 2)), dma((16, 2)),
             dma((9, 2, 2)), dma((9, 2)), dma((3,)), dma((3,)),
             dma((NZ, NZ - 1)), dma((NZ, NZ - 1)), dma((NX, N_ROW)), dma((NX, N_ROW))],
         compiler_params=pltpu.CompilerParams(collective_id=0, has_side_effects=True, vmem_limit_bytes=VMEM_LIMIT),

time: 67.2 us -> 62.7 us (0.933)
  Pallas kernels: 63.7 us -> 59.3 us
    pallas_call x1, Pallas kernels: 63.7 us -> 59.3 us  [local(): pl.pallas_call(merged_kernel, out_shape=(shape(1, BLK), shape(1, BLK), sh...]
where the time goes in v2:
time: 62.7 us; the launch traced here: 62.6 us
  Pallas kernels  59.3 us (95%)
  between operations  1.97 us (3%)
  local copies, waits for them, and re-layouts  1.13 us (2%)
    pallas_call x1, Pallas kernels, local(): pl.pallas_call(merged_kernel, out_shape=(shape(1, BLK), shape(1, BLK), sh...  59.3 us

profile of v2, /device:TPU:1, one launch (start us, length us, event | category | flops | bytes accessed | tf_op | source)
XLA Modules:
  0.0 62.6 jit_solution(14219863594334316744)
XLA Ops:
  1.3 59.3 %shard_map.95 = (f32[1,256]{1,0:T(1,128)S(1)}, f32[1,256]{1,0:T(1,128)S(1)}, f32[1,128]{1,0:T(1,128)}) custom-call(s32[64]{0:T(128)} %src_in.1, s32[64]{0:T(128)} %tgt_in.1, s32[1]{0:T(128)S(6)} %copy.20.count_in, f32[256,256]{1,0:T(8,128)} %src_ref.1, f32[256,256]{1,0:T(8,128)} %tgt_ref.1, f32[1,256]{1,0:T(1,128)} %bitcast.23, f32[1,256]{1,0:T(1,128)} %bitcast.25, ...), custom_call_target="tpu_custom_call" | custom-call | tf_op jit(solution)/shard_map/pallas_call | solution.py:799
  61.2 0.2 conditional.1
  61.5 0.6 copy.21
  62.0 0.6 copy.22

commit v3 on v2

--- a/solution.py
+++ b/solution.py
@@ -71,7 +71,7 @@
     return [(OTHER_WAY[name], mirror(target)) for name, target in sends_of(*mirror(pos))]
 
 
-PARTS = ((0, 128), (128, 136))
+PARTS = ((0, 160), (160, 104))
 STEPS = (
     ("X", 0), ("Y", 0, 0), ("M", 0, 0), ("y", 1, 0, 0), ("y", 0, 1, 0), ("z", 1, 0), ("y", 0, 3, 0), ("y", 3, 0, 0),
     ("z", -1, 0), ("y", 1, 0, 1), ("y", 0, 1, 1), ("z", 1, 1), ("y", 0, 3, 1), ("y", 3, 0, 1), ("z", -1, 1), ("X", 1),
@@ -407,7 +407,7 @@
 
 
 def merged_kernel(src_in, tgt_in, count_in, src_ref, tgt_ref, pot_ref, mass_ref, mass_b_in,
-                  f_out, g_out, bad_out,
+                  both_out, bad_out,
                   y_raw, x_raw, y3, x3, bias, top, total, scores, col_top, col_sum, tabs, tab_s, mine, src_list, tgt_list, count_ref, mass_b_ref, row_out, row_logs, row_got,
                   col_out, col_got,
                   load_sem, send_sem, recv_sem, mate_send, mate_recv, z_send, z_recv, l_send, l_recv,
@@ -706,7 +706,7 @@
     f_square = jnp.broadcast_to(jnp.sum(f_square * f_square, axis=1, keepdims=True), (BLK, 128)).T[0:1]
     g_square = y_raw[x, row, pl.ds(0, BLK), :]
     g_square = jnp.broadcast_to(jnp.sum(g_square * g_square, axis=1, keepdims=True), (BLK, 128)).T[0:1]
-    f_out[...] = (ENTROPY * x_raw[z, pl.ds(BLK, 1), :] - (ENTROPY * LN2) * row_logs[pl.ds(z, 1), :]
+    both_out[pl.ds(0, 1), :] = (ENTROPY * x_raw[z, pl.ds(BLK, 1), :] - (ENTROPY * LN2) * row_logs[pl.ds(z, 1), :]
                   + f_square * (1.0 / D))
     col_got[x, row] = col_out[x, row]
     for away in (2, 1, 3, 0):
@@ -717,7 +717,7 @@
     every = col_got[...].reshape(NX * N_ROW, 1, BLK + 128)
     high = jnp.max(every[:, :, :BLK], axis=0)
     whole = jnp.sum(jnp.exp2(every[:, :, :BLK] - high[None]), axis=0)
-    g_out[...] = (ENTROPY * mass_b_ref[...] - (ENTROPY * LN2) * (high + jnp.log2(whole)) + g_square * (1.0 / D))
+    both_out[pl.ds(1, 1), :] = (ENTROPY * mass_b_ref[...] - (ENTROPY * LN2) * (high + jnp.log2(whole)) + g_square * (1.0 / D))
     bad_out[...] = jnp.max(every[:, :, BLK:], axis=0)
 
     def sent(b, carry):
@@ -796,11 +796,11 @@
     dma = pltpu.SemaphoreType.DMA
     vmem = pltpu.VMEM
     f32 = jnp.float32
-    f_own, g_own, bad = pl.pallas_call(
+    both, bad = pl.pallas_call(
         merged_kernel,
-        out_shape=(shape(1, BLK), shape(1, BLK), shape(1, 128)),
+        out_shape=(shape(2, BLK), shape(1, 128)),
         in_specs=[anywhere] * 8,
-        out_specs=(whole, whole, whole),
+        out_specs=(whole, whole),
         scratch_shapes=[
             vmem((NX, N_ROW, ROWS, D), f32), vmem((NZ, ROWS, D), f32),
             vmem((NX, N_ROW, BLK, 3 * D), jnp.bfloat16), vmem((NZ, BLK, 3 * D), jnp.bfloat16),
@@ -816,7 +816,8 @@
         compiler_params=pltpu.CompilerParams(collective_id=0, has_side_effects=True, vmem_limit_bytes=VMEM_LIMIT),
     )(src_block, tgt_block, pair_count, sources, targets, g_pot[None], log_a[None], log_b[None])
     args = (sources, targets, g_pot, log_a, log_b, src_block, tgt_block, pair_count)
-    return lax.cond(bad[0, 0] > 0.5, lambda: general(*args), lambda: (f_own.reshape(BLK), g_own.reshape(BLK)))
+    both = lax.cond(bad[0, 0] > 0.5, lambda: jnp.stack(general(*args)), lambda: both)
+    return both[0], both[1]
 
 
 def solution(mesh):

time: 62.7 us -> 60.4 us (0.963)
  Pallas kernels: 59.3 us -> 57.5 us
    pallas_call x1, Pallas kernels: 59.3 us -> 57.5 us  [local(): pl.pallas_call(merged_kernel, out_shape=(shape(2, BLK), shape(1, 128)), i...]
    unnamed x2 -> x0, local copies, waits for them, and re-layouts: 1.13 us -> none
where the time goes in v3:
time: 60.4 us; the launch traced here: 60.3 us
  Pallas kernels  57.5 us (95%)
  between operations  1.92 us (3%)
    pallas_call x1, Pallas kernels, local(): pl.pallas_call(merged_kernel, out_shape=(shape(2, BLK), shape(1, 128)), i...  57.5 us

profile of v3, /device:TPU:1, one launch (start us, length us, event | category | flops | bytes accessed | tf_op | source)
XLA Modules:
  0.0 60.3 jit_solution(5896084031558814220)
XLA Ops:
  1.3 57.5 %shard_map.95 = (f32[2,256]{1,0:T(2,128)S(1)}, f32[1,128]{1,0:T(1,128)}) custom-call(s32[64]{0:T(128)} %src_in.1, s32[64]{0:T(128)} %tgt_in.1, s32[1]{0:T(128)S(6)} %copy.14.count_in, f32[256,256]{1,0:T(8,128)} %src_ref.1, f32[256,256]{1,0:T(8,128)} %tgt_ref.1, f32[1,256]{1,0:T(1,128)} %bitcast.21, f32[1,256]{1,0:T(1,128)} %bitcast.23, f32[1,256]{1,0:T(1,128)} %bitcast.25), custom_call_target="tpu_custom_call" | custom-call | tf_op jit(solution)/shard_map/pallas_call | solution.py:799
  59.5 0.2 conditional.1
  59.7 0.6 fusion.1

commit v4 on v3

--- a/solution.py
+++ b/solution.py
@@ -83,7 +83,7 @@
     ("y", 3, 1, 1), ("Y", 3, 1), ("Y", 2, 3), ("D", 0, 1), ("z", -3, 1), ("z", 3, 1), ("y", 3, 2, 0), ("y", 2, 1, 0),
     ("X", 3), ("X", -3), ("M", 2, 3), ("M", 3, 1), ("D", -1, 2), ("z", 4, 0), ("y", 1, 2, 0), ("y", 1, 2, 1),
     ("Y", 1, 2), ("D", -2, 3), ("y", 2, 2, 0), ("y", 2, 1, 1), ("Y", 2, 1), ("z", 4, 1), ("X", 4), ("D", -3, 4),
-    ("M", 1, 2), ("y", 3, 2, 1), ("y", 2, 2, 1), ("Y", 3, 2), ("Y", 2, 2), ("M", 2, 1), ("M", 3, 2), ("M", 2, 2),
+    ("M", 1, 2), ("y", 3, 2, 1), ("y", 2, 2, 1), ("Y", 3, 2), ("Y", 2, 2), ("M", 2, 1), ("M", 3, 2),
 )
 
 
@@ -614,25 +614,37 @@
         return remote(row_out.at[b], row_got.at[b, n - 1], row_send.at[b, n - 1], row_recv.at[b, n - 1],
                       device(y, k, x, lax.rem(z + n, NZ)))
 
-    def close(b):
+    def sums_of(b):
         high = jnp.max(top[b], axis=1, keepdims=True)
         whole = jnp.sum(total[b] * jnp.exp2(top[b] - high), axis=1, keepdims=True)
-        logs = jnp.where(whole > 0.0, high + jnp.log2(whole), LOWEST)
-        row_out[b, :, pl.ds(0, BLK)] = jnp.broadcast_to(logs, (BLK, 128)).T[0:1]
-        row_out[b, :, pl.ds(BLK, 128)] = bad
-
-    def far(i, carry):
-        for away in (1, 3, 2):
+        return jnp.where(whole > 0.0, high + jnp.log2(whole), LOWEST)
+
+    first_half = lax.broadcasted_iota(jnp.int32, (BLK, 128), 1) < 64
+
+    def pairs_with(i, groups):
+        for away in groups:
             for b in (2 * i, 2 * i + 1):
                 pair(wrap4(x + away), b)
-        for b in (2 * i, 2 * i + 1):
-            close(b)
+
+    def leave(i):
+        both_sums = jnp.where(first_half, sums_of(2 * i), sums_of(2 * i + 1)).T
+        for n in (0, 1):
+            row_out[2 * i + n, :, pl.ds(0, BLK)] = both_sums[64 * n:64 * n + 1]
+            row_out[2 * i + n, :, pl.ds(BLK, 128)] = bad
         for b in (2 * i, 2 * i + 1):
             for n in range(1, NZ):
                 row_copy(b, n).start()
+
+    def far(i, carry):
+        pairs_with(i, (1, 3, 2))
+        leave(i)
         return carry
 
-    lax.fori_loop(0, NZ // 2, far, 0)
+    pairs_with(0, (1, 3))
+    prep_mate(2, 2)
+    pairs_with(0, (2,))
+    leave(0)
+    lax.fori_loop(1, NZ // 2, far, 0)
 
     def rows_of(b, bad):
         for n in range(1, NZ):
@@ -718,7 +730,7 @@
     high = jnp.max(every[:, :, :BLK], axis=0)
     whole = jnp.sum(jnp.exp2(every[:, :, :BLK] - high[None]), axis=0)
     both_out[pl.ds(1, 1), :] = (ENTROPY * mass_b_ref[...] - (ENTROPY * LN2) * (high + jnp.log2(whole)) + g_square * (1.0 / D))
-    bad_out[...] = jnp.max(every[:, :, BLK:], axis=0)
+    bad_out[0, 0] = jnp.max(every[:, :, BLK:])
 
     def sent(b, carry):
         for n in range(1, NZ):
@@ -798,9 +810,9 @@
     f32 = jnp.float32
     both, bad = pl.pallas_call(
         merged_kernel,
-        out_shape=(shape(2, BLK), shape(1, 128)),
+        out_shape=(shape(2, BLK), shape(1, 1)),
         in_specs=[anywhere] * 8,
-        out_specs=(whole, whole),
+        out_specs=(whole, pl.BlockSpec(memory_space=pltpu.SMEM)),
         scratch_shapes=[
             vmem((NX, N_ROW, ROWS, D), f32), vmem((NZ, ROWS, D), f32),
             vmem((NX, N_ROW, BLK, 3 * D), jnp.bfloat16), vmem((NZ, BLK, 3 * D), jnp.bfloat16),

time: 60.4 us -> 60.3 us (level)
  no operation moved by 1% of the time
where the time goes in v4:
time: 60.3 us; the launch traced here: 60.2 us
  Pallas kernels  57.7 us (96%)
  between operations  1.92 us (3%)
    pallas_call x1, Pallas kernels, local(): pl.pallas_call(merged_kernel, out_shape=(shape(2, BLK), shape(1, 1)), in_...  57.7 us

profile of v4, /device:TPU:1, one launch (start us, length us, event | category | flops | bytes accessed | tf_op | source)
XLA Modules:
  0.0 60.2 jit_solution(16960367126168686283)
XLA Ops:
  1.3 57.7 %shard_map.95 = (f32[2,256]{1,0:T(2,128)S(1)}, f32[1,1]{1,0:T(1,128)}) custom-call(s32[64]{0:T(128)} %src_in.1, s32[64]{0:T(128)} %tgt_in.1, s32[1]{0:T(128)S(6)} %copy.14.count_in, f32[256,256]{1,0:T(8,128)} %src_ref.1, f32[256,256]{1,0:T(8,128)} %tgt_ref.1, f32[1,256]{1,0:T(1,128)} %bitcast.20, f32[1,256]{1,0:T(1,128)} %bitcast.22, f32[1,256]{1,0:T(1,128)} %bitcast.24), custom_call_target="tpu_custom_call" | custom-call | tf_op jit(solution)/shard_map/pallas_call | solution.py:811
  59.7 0.6 fusion.1
  (1 shorter events, 0.0 us)
